TPU v7x, 512 devices: a whole 4x8x8 slice. The times are simulated.
512 devices in a mesh: rep: 32 (over z, x), shard: 16 (over y, core).
Axes of the slice: x: 4, y: 8, z: 8, core: 2. Of those that a mesh axis runs over, the one named last changes fastest.
Arguments:
- grads: float32 [32, 32, 32, 5120], P('rep', 'shard'), may hold values from -1000 to 1000
- weight: float32 [32, 32, 5120], P('shard'), may hold values from -6 to 6
- moment_one: float32 [32, 32, 5120], P('shard', 'rep'), may hold values from -6 to 6
- moment_two: float32 [32, 32, 5120], P('shard', 'rep'), may hold values from 0.1 to 3
Outputs:
- new_weight: float32 [32, 32, 5120], P('shard')
- new_moment_one: float32 [32, 32, 5120], P('shard', 'rep')
- new_moment_two: float32 [32, 32, 5120], P('shard', 'rep')
All inputs are finite; a program needn't handle non-finite values.
Results may differ from a plain program's by a relative error of at most 0.0003.
Values sent between devices are 32-bit elements; how exact they have to be, the bound alone decides.
A program may use at most 64 MiB of HBM per device.

v0:
```python
import jax
import jax.numpy as jnp
from jax import lax
from jax.sharding import PartitionSpec as P

STEP = 100


def trimmed_block(block, trim_count):
    count = block.shape[0]
    order = jnp.arange(count, dtype=jnp.int32)
    lower = block[None, :, :] < block[:, None, :]
    equal = (block[None, :, :] == block[:, None, :]) & (order[None, :, None] < order[:, None, None])
    rank = jnp.sum((lower | equal).astype(jnp.int32), axis=1)
    keep = (rank >= trim_count) & (rank < count - trim_count)
    kept = jnp.sum(jnp.where(keep, block, jnp.zeros_like(block)), axis=0)
    return kept / (count - 2 * trim_count)


def trimmed_mean(values, trim_count):
    count, total = values.shape
    width = 512
    blocks = values.reshape(count, total // width, width).transpose(1, 0, 2)
    result = lax.map(lambda item: trimmed_block(item, trim_count), blocks)
    return result.reshape(total)


def trimmed_rows(received):
    count = received.shape[0]
    flat = received.reshape(count, -1)
    return trimmed_mean(flat, count // 8).reshape(received.shape[1:])


def on_device(grads, weight, moment_one, moment_two):
    params = weight.shape[0] * lax.axis_size("shard") * weight.shape[1] * weight.shape[2]
    received = lax.all_to_all(grads, "rep", split_axis=2, concat_axis=0, tiled=True)
    trimmed = trimmed_rows(received)
    squares = jnp.sum(trimmed * trimmed)
    total = lax.psum(squares, ("rep", "shard"))
    factor = jnp.minimum(1.0, 1.0 / jnp.sqrt(total / params + 1e-12))
    clipped = factor * trimmed
    new_one = 0.9 * moment_one + 0.1 * clipped
    new_two = 0.95 * moment_two + 0.05 * clipped * clipped
    update = new_one / (1.0 - 0.9**STEP) / (jnp.sqrt(new_two / (1.0 - 0.95**STEP)) + 1e-08)
    owned = lax.dynamic_slice_in_dim(
        weight, lax.axis_index("rep") * moment_one.shape[1], moment_one.shape[1], 1
    )
    owned_new = owned - 0.05 * (update + 0.1 * owned)
    new_weight = lax.all_gather(owned_new, "rep", axis=1, tiled=True)
    return (new_weight, new_one, new_two)


def solution(mesh):
    return jax.shard_map(
        on_device,
        mesh=mesh,
        in_specs=(
            P("rep", "shard", None, None),
            P("shard", None, None),
            P("shard", "rep", None),
            P("shard", "rep", None),
        ),
        out_specs=(P("shard", None, None), P("shard", "rep", None), P("shard", "rep", None)),
        check_vma=False,
    )
```

profile of v0, /device:TPU:6, one launch (start us, length us, event | category | flops | bytes accessed | tf_op | source)
XLA Modules:
  0.0 285.1 jit_solution(3444203935370994533)
XLA Ops:
  7.2 3.5 %copy.19 = f32[1,2,32,5120]{3,1,0,2:T(2,128)} copy(f32[1,2,32,5120]{3,2,1,0:T(8,128)} %param.6) | data formatting | bytes 2621440 | tf_op args[0]
  10.7 13.4 %all-to-all-start = ((f32[1,2,32,5120]{3,1,0,2:T(2,128)}), f32[1,2,32,5120]{3,1,0,2:T(2,128)S(1)}, u32[]{:S(2)}, u32[]{:S(2)}) async-start(f32[1,2,32,5120]{3,1,0,2:T(2,128)} %copy.19), calls=%async_computation | async-start | bytes 2621440 | tf_op jit(solution)/shard_map/all_to_all | solution.py:36
  24.1 33.6 %all-to-all-done = f32[1,2,32,5120]{3,1,0,2:T(2,128)S(1)} async-done(((f32[1,2,32,5120]{3,1,0,2:T(2,128)}), f32[1,2,32,5120]{3,1,0,2:T(2,128)S(1)}, u32[]{:S(2)}, u32[]{:S(2)}) %all-to-all-start) | async-done | bytes 1310752 | tf_op jit(solution)/shard_map/all_to_all | solution.py:36
  57.8 2.2 reshape_reshape.4
  60.0 39.4 %while.10 = (s32[]{:T(128)}, f32[20,512]{1,0:T(8,128)S(1)}, f32[20,32,512]{2,0,1:T(8,128)}, s32[]{:T(128)}, s32[]{:T(128)}) while((s32[]{:T(128)}, f32[20,512]{1,0:T(8,128)S(1)}, f32[20,32,512]{2,0,1:T(8,128)}, s32[]{:T(128)}, s32[]{:T(128)}) %tuple.34), condition=%wide.region_3.4_spmd, body=%wide.region_0.3_spmd.sunk | while | flops 3212290 | bytes 536645 | solution.py:24
  60.0 1.1 constant_dynamic-slice_fusion.3
  61.1 0.7 convert_reduce_fusion.2
  61.9 0.1 dynamic_update_slice.5
  61.9 1.1 constant_dynamic-slice_fusion.3
  63.1 0.7 convert_reduce_fusion.2
  63.8 0.1 dynamic_update_slice.5
  63.9 1.1 constant_dynamic-slice_fusion.3
  65.0 0.7 convert_reduce_fusion.2
  65.9 1.1 constant_dynamic-slice_fusion.3
  67.0 0.7 convert_reduce_fusion.2
  67.8 0.1 dynamic_update_slice.5
  67.9 1.1 constant_dynamic-slice_fusion.3
  69.0 0.7 convert_reduce_fusion.2
  69.8 0.1 dynamic_update_slice.5
  69.8 1.1 constant_dynamic-slice_fusion.3
  71.0 0.7 convert_reduce_fusion.2
  71.8 1.1 constant_dynamic-slice_fusion.3
  72.9 0.7 convert_reduce_fusion.2
  73.7 0.1 dynamic_update_slice.5
  73.8 1.1 constant_dynamic-slice_fusion.3
  74.9 0.7 convert_reduce_fusion.2
  75.8 1.1 constant_dynamic-slice_fusion.3
  76.9 0.7 convert_reduce_fusion.2
  77.6 0.1 dynamic_update_slice.5
  77.7 1.1 constant_dynamic-slice_fusion.3
  78.9 0.7 convert_reduce_fusion.2
  79.6 0.1 dynamic_update_slice.5
  79.7 1.1 constant_dynamic-slice_fusion.3
  80.8 0.7 convert_reduce_fusion.2
  81.7 1.1 constant_dynamic-slice_fusion.3
  82.8 0.7 convert_reduce_fusion.2
  83.6 0.1 dynamic_update_slice.5
  83.6 1.1 constant_dynamic-slice_fusion.3
  84.8 0.7 convert_reduce_fusion.2
  85.6 1.1 constant_dynamic-slice_fusion.3
  86.7 0.7 convert_reduce_fusion.2
  87.5 0.1 dynamic_update_slice.5
  87.6 1.1 constant_dynamic-slice_fusion.3
  88.7 0.7 convert_reduce_fusion.2
  89.6 1.1 constant_dynamic-slice_fusion.3
  90.7 0.7 convert_reduce_fusion.2
  91.5 0.1 dynamic_update_slice.5
  91.5 1.1 constant_dynamic-slice_fusion.3
  92.7 0.7 convert_reduce_fusion.2
  93.4 0.1 dynamic_update_slice.5
  93.5 1.1 constant_dynamic-slice_fusion.3
  94.6 0.7 convert_reduce_fusion.2
  95.5 1.1 constant_dynamic-slice_fusion.3
  96.6 0.7 convert_reduce_fusion.2
  97.4 0.1 dynamic_update_slice.5
  97.5 1.1 constant_dynamic-slice_fusion.3
  98.6 0.7 convert_reduce_fusion.2
  99.4 0.6 multiply_reduce_fusion
  100.1 95.5 %psum.7 = f32[]{:T(128)} all-reduce(f32[]{:T(128)} %multiply_reduce_fusion), channel_id=1, replica_groups=mesh['rep'=32,'shard'=16] {'rep','shard'}, use_global_device_ids=true, to_apply=%region_5.6 | all-reduce | flops 1 | bytes 8 | tf_op jit(solution)/shard_map/psum | solution.py:39
  196.3 0.8 multiply_subtract_fusion
  197.1 0.7 copy.23
  197.8 0.7 copy.24
  198.5 77.0 %all-gather.2.cloned.1.call-done = f32[2,32,5120]{2,0,1:T(2,128)} async-done(((f32[2,1,5120]{2,0,1:T(2,128)}), f32[2,32,5120]{2,0,1:T(2,128)}) %all-gather.2.cloned.1.call-update) | async-done | bytes 1310736 | tf_op jit(solution)/shard_map/all_gather | solution.py:49
  275.4 2.8 copy.22
  (100 shorter events, 1.6 us)
Async XLA Ops:
  7.2 92.9 %copy-start = (f32[2,32,5120]{2,1,0:T(8,128)S(1)}, f32[2,32,5120]{2,1,0:T(8,128)}, u32[]{:S(2)}) copy-start(f32[2,32,5120]{2,1,0:T(8,128)} %param.7) | copy-start | bytes 3932164
  10.7 47.1 %all-to-all-start = ((f32[1,2,32,5120]{3,1,0,2:T(2,128)}), f32[1,2,32,5120]{3,1,0,2:T(2,128)S(1)}, u32[]{:S(2)}, u32[]{:S(2)}) async-start(f32[1,2,32,5120]{3,1,0,2:T(2,128)} %copy.19), calls=%async_computation | async-start | bytes 2621440 | tf_op jit(solution)/shard_map/all_to_all | solution.py:36
  24.1 251.3 %all-gather.2.cloned.1.call-start = ((), (), s32[]{:S(2)}) async-start(), calls=%async_computation.1 | async-start | bytes 1351680 | tf_op jit(solution)/shard_map/all_gather | solution.py:49
  60.0 136.4 %copy-start.1 = (f32[2,1,5120]{2,1,0:T(1,128)S(1)}, f32[2,1,5120]{2,1,0:T(1,128)}, u32[]{:S(2)}) copy-start(f32[2,1,5120]{2,1,0:T(1,128)} %param.8) | copy-start | bytes 122884
  60.0 136.4 %copy-start.2 = (f32[2,1,5120]{2,1,0:T(1,128)S(1)}, f32[2,1,5120]{2,1,0:T(1,128)}, u32[]{:S(2)}) copy-start(f32[2,1,5120]{2,1,0:T(1,128)} %param.9) | copy-start | bytes 122884
Sparse Core Ops, SparseCore 0:
  197.3 78.1 all-gather.1
where the time goes:
time: 287 us; the launch traced here: 285 us
  waiting for transfers between devices  111 us (39%)
  blocking collectives  95.5 us (33%)
  local copies, waits for them, and re-layouts  33.2 us (12%)
  other arithmetic  16.5 us (6%)
  between operations  14.8 us (5%)
  starting transfers between devices  13.4 us (5%)
    psum x1, blocking collectives, on_device(): total = lax.psum(squares, ('rep', 'shard'))  95.5 us
    all_gather x1, waiting for transfers between devices, on_device(): new_weight = lax.all_gather(owned_new, 'rep', axis=1, tiled=True)  77 us
    all_to_all x1, waiting for transfers between devices, on_device(): lax.all_to_all(grads, 'rep', split_axis=2, concat_axis=0, tiled=True)  33.6 us
    dynamic_slice x40, local copies, waits for them, and re-layouts, trimmed_mean(): result = lax.map(lambda item: trimmed_block(item, trim_count), blocks)  22.1 us
    reduce_sum x20, other arithmetic, trimmed_block(): rank = jnp.sum((lower | equal).astype(jnp.int32), axis=1)  14.3 us
    all_to_all x1, starting transfers between devices, on_device(): lax.all_to_all(grads, 'rep', split_axis=2, concat_axis=0, tiled=True)  13.4 us
    unnamed x10, local copies, waits for them, and re-layouts  7.62 us
  transfers between devices with their start and end apart: 2, of which 2 were waited for; matrix products, arithmetic and copies ran while one was open for 0% of the time, Pallas kernels for 0%

commit v1 on v0

v1 whole, which is shorter than its diff:
```python
import jax
import jax.numpy as jnp
from jax import lax
from jax.experimental import pallas as pl
from jax.experimental.pallas import tpu as pltpu
from jax.sharding import PartitionSpec as P

STEP = 100
MESH = pl.DeviceIdType.MESH
NZ, NX = 8, 4
REPS, SHARDS = 32, 16
TRIM = 4
F32 = jnp.float32

SORT8 = (
    (0, 1), (2, 3), (4, 5), (6, 7),
    (0, 2), (1, 3), (4, 6), (5, 7),
    (1, 2), (5, 6),
    (0, 4), (1, 5), (2, 6), (3, 7),
    (2, 4), (3, 5),
    (1, 2), (3, 4), (5, 6),
)


def exchange(values, i, j):
    a, b = values[i], values[j]
    values[i], values[j] = jnp.minimum(a, b), jnp.maximum(a, b)


def sort8(values):
    values = list(values)
    for i, j in SORT8:
        exchange(values, i, j)
    return values[:4], values[4:]


def add_all(values):
    values = list(values)
    while len(values) > 1:
        values = [a + b for a, b in zip(values[::2], values[1::2])] + (
            [values[-1]] if len(values) % 2 else []
        )
    return values[0]


def merge(one, two):
    (low_a, high_a), (low_b, high_b) = one, two
    low = [jnp.minimum(low_a[i], low_b[3 - i]) for i in range(4)]
    high = [jnp.maximum(high_a[i], high_b[3 - i]) for i in range(4)]
    for i, j in ((0, 2), (1, 3), (0, 1), (2, 3)):
        exchange(low, i, j)
        exchange(high, i, j)
    return (low, high), middle(one, two)


def middle(one, two):
    (low_a, high_a), (low_b, high_b) = one, two
    return add_all(
        [jnp.maximum(low_a[i], low_b[3 - i]) for i in range(4)]
        + [jnp.minimum(high_a[i], high_b[3 - i]) for i in range(4)]
    )


def kept_sum(values):
    groups = [sort8(values[8 * g : 8 * g + 8]) for g in range(4)]
    left, left_sum = merge(groups[0], groups[1])
    right, right_sum = merge(groups[2], groups[3])
    return left_sum + right_sum + middle(left, right)


def row_of(ref, r):
    return ref.at[:, r // 8, :, lax.rem(r, 8), :]


def tiles(block):
    return block.reshape(2, 4, 8, 40, 128).transpose(0, 1, 3, 2, 4)


def kernel(
    params,
    grads,
    weight,
    one_ref,
    two_ref,
    new_weight,
    new_one_ref,
    new_two_ref,
    received,
    row,
    outgoing,
    trimmed,
    partial,
    sums,
    local_sem,
    send_sem,
    recv_sem,
    sum_send,
    sum_recv,
    gather_send,
    z_recv,
    x_recv,
    half_recv,
    out_sem,
):
    me = lax.axis_index("rep")
    shard = lax.axis_index("shard")
    z, x = me // NX, lax.rem(me, NX)

    def at(dz, dx):
        return lax.rem(z + dz, NZ) * NX + lax.rem(x + dx, NX)

    own_row = pltpu.make_async_copy(row_of(weight, me), row, local_sem.at[0])
    own_row.start()
    own_grads = pltpu.make_async_copy(
        row_of(grads, me), received.at[me], local_sem.at[1]
    )
    own_grads.start()

    barrier = pltpu.get_barrier_semaphore()
    for i in range(1, REPS):
        pl.semaphore_signal(
            barrier, inc=1, device_id=(lax.rem(me + i, REPS), shard), device_id_type=MESH
        )
    for i in range(1, SHARDS):
        pl.semaphore_signal(
            barrier, inc=1, device_id=(me, lax.rem(shard + i, SHARDS)), device_id_type=MESH
        )
    pl.semaphore_wait(barrier, REPS + SHARDS - 2)

    for dz in (4, 3, 5, 2, 6, 1, 7, 0):
        for dx in (2, 1, 3, 0):
            if dz or dx:
                peer = at(dz, dx)
                pltpu.make_async_remote_copy(
                    src_ref=row_of(grads, peer),
                    dst_ref=received.at[me],
                    send_sem=send_sem,
                    recv_sem=recv_sem,
                    device_id=(peer, shard),
                    device_id_type=MESH,
                ).start()
    own_row.wait()
    own_grads.wait()
    others = received.at[pl.ds(0, REPS - 1)]
    pltpu.make_async_copy(others, others, recv_sem).wait()

    def block(j, squares):
        h, rows = j // 5, pl.ds(pl.multiple_of(lax.rem(j, 5) * 8, 8), 8)
        mean = kept_sum([received[i, h, rows, :] for i in range(REPS)]) / (REPS - 2 * TRIM)
        trimmed[h, rows, :] = mean
        return squares + mean * mean

    squares = lax.fori_loop(0, 10, block, jnp.zeros((8, 128), F32))
    total = jnp.sum(squares, axis=0, keepdims=True)

    for stage, (count, mine, device) in enumerate(
        (
            (REPS, me, lambda p: (p, shard)),
            (SHARDS, shard, lambda p: (me, p)),
        )
    ):
        partial[stage] = total
        sums[stage, pl.ds(mine, 1), :] = total
        for i in range(1, count):
            pltpu.make_async_remote_copy(
                src_ref=partial.at[stage],
                dst_ref=sums.at[stage, pl.ds(mine, 1), :],
                send_sem=sum_send.at[stage],
                recv_sem=sum_recv.at[stage],
                device_id=device(lax.rem(mine + i, count)),
                device_id_type=MESH,
            ).start()
        got = sums.at[stage, pl.ds(0, count - 1), :]
        pltpu.make_async_copy(got, got, sum_recv.at[stage]).wait()
        total = jnp.sum(sums[stage, 0:count, :], axis=0, keepdims=True)
    total = jnp.sum(total, axis=1, keepdims=True)
    factor = jnp.minimum(1.0, 1.0 / jnp.sqrt(total / params + 1e-12))

    clipped = factor * trimmed[...]
    new_one = 0.9 * one_ref[...] + 0.1 * clipped
    new_two = 0.95 * two_ref[...] + 0.05 * clipped * clipped
    update = new_one / (1.0 - 0.9**STEP) / (jnp.sqrt(new_two / (1.0 - 0.95**STEP)) + 1e-08)
    owned = row[...]
    outgoing[...] = owned - 0.05 * (update + 0.1 * owned)
    new_one_ref[...] = new_one
    new_two_ref[...] = new_two

    def at_row(r):
        return row_of(new_weight, r)

    def push(src, r, peer, sem):
        pltpu.make_async_remote_copy(
            src_ref=src,
            dst_ref=at_row(r),
            send_sem=gather_send,
            recv_sem=sem,
            device_id=(peer, shard),
            device_id_type=MESH,
        ).start()

    for dz in (1, 7, 2, 6, 3, 5, 4):
        push(outgoing, me, at(dz, 0), z_recv.at[z])
    for side, dx in enumerate((1, 3)):
        push(outgoing, me, at(0, dx), x_recv.at[side, z])
    keep = pltpu.make_async_copy(outgoing, at_row(me), out_sem)
    keep.start()

    def from_x(dz):
        zz = lax.rem(z + dz, NZ)
        for side, dx in enumerate((1, 3)):
            r = at(dz, NX - dx)
            view = at_row(r)
            pltpu.make_async_copy(view, view, x_recv.at[side, zz]).wait()
            half = new_weight.at[side, r // 8, :, lax.rem(r, 8), :]
            pltpu.make_async_remote_copy(
                src_ref=half,
                dst_ref=half,
                send_sem=gather_send,
                recv_sem=half_recv,
                device_id=(at(0, dx), shard),
                device_id_type=MESH,
            ).start()

    order = (0, 1, 7, 2, 6, 3, 5, 4)
    for k, dz in enumerate(order[1:]):
        zz = lax.rem(z + dz, NZ)
        r = at(dz, 0)
        view = at_row(r)
        pltpu.make_async_copy(view, view, z_recv.at[zz]).wait()
        for side, dx in enumerate((1, 3)):
            push(view, r, at(0, dx), x_recv.at[side, zz])
        from_x(order[k])
    from_x(order[-1])
    eight = received.at[pl.ds(0, 8)]
    pltpu.make_async_copy(eight, eight, half_recv).wait()
    keep.wait()

    pltpu.make_async_copy(others, others, send_sem).wait()
    pltpu.make_async_copy(others, others, gather_send).wait()
    for stage, count in enumerate((REPS, SHARDS)):
        got = sums.at[stage, pl.ds(0, count - 1), :]
        pltpu.make_async_copy(got, got, sum_send.at[stage]).wait()


def on_device(grads, weight, moment_one, moment_two):
    params = weight.shape[0] * SHARDS * weight.shape[1] * weight.shape[2]
    vmem = pl.BlockSpec(memory_space=pltpu.VMEM)
    hbm = pl.BlockSpec(memory_space=pltpu.HBM)
    unit = (2, 40, 128)
    dma = pltpu.SemaphoreType.DMA
    new_weight, new_one, new_two = pl.pallas_call(
        lambda *refs: kernel(params, *refs),
        name="robust_step",
        out_shape=(
            jax.ShapeDtypeStruct((2, 4, 40, 8, 128), F32),
            jax.ShapeDtypeStruct(unit, F32),
            jax.ShapeDtypeStruct(unit, F32),
        ),
        in_specs=[hbm, hbm, vmem, vmem],
        out_specs=(vmem, vmem, vmem),
        scratch_shapes=[
            pltpu.VMEM((REPS,) + unit, F32),
            pltpu.VMEM(unit, F32),
            pltpu.VMEM(unit, F32),
            pltpu.VMEM(unit, F32),
            pltpu.VMEM((2, 1, 128), F32),
            pltpu.VMEM((2, REPS, 128), F32),
            dma((2,)),
            dma,
            dma,
            dma((2,)),
            dma((2,)),
            dma,
            dma((NZ,)),
            dma((2, NZ)),
            dma,
            dma,
        ],
        compiler_params=pltpu.CompilerParams(
            collective_id=0, has_side_effects=True
        ),
    )(tiles(grads[0]), tiles(weight), moment_one.reshape(unit), moment_two.reshape(unit))
    return (
        new_weight.transpose(0, 1, 3, 2, 4).reshape(weight.shape),
        new_one.reshape(moment_one.shape),
        new_two.reshape(moment_two.shape),
    )


def solution(mesh):
    return jax.shard_map(
        on_device,
        mesh=mesh,
        in_specs=(
            P("rep", "shard", None, None),
            P("shard", None, None),
            P("shard", "rep", None),
            P("shard", "rep", None),
        ),
        out_specs=(P("shard", None, None), P("shard", "rep", None), P("shard", "rep", None)),
        check_vma=False,
    )
```

time: 287 us -> 85.7 us (0.30)
  waiting for transfers between devices: 111 us -> 0 us
  blocking collectives: 95.5 us -> 0 us
  Pallas kernels: 0 us -> 81 us
  local copies, waits for them, and re-layouts: 33.2 us -> 3.73 us
  other arithmetic: 16.5 us -> 0 us
  between operations: 14.8 us -> 0.66 us
  starting transfers between devices: 13.4 us -> 0 us
    psum x1 -> x0, blocking collectives: 95.5 us -> none  [on_device(): total = lax.psum(squares, ('rep', 'shard'))]
    pallas_call x0 -> x1, Pallas kernels: none -> 81 us  [on_device(): pl.pallas_call(lambda *refs: kernel(params, *refs), name='robust_step', o...]
    all_gather x1 -> x0, waiting for transfers between devices: 77 us -> none  [on_device(): new_weight = lax.all_gather(owned_new, 'rep', axis=1, tiled=True)]
    all_to_all x1 -> x0, waiting for transfers between devices: 33.6 us -> none  [on_device(): lax.all_to_all(grads, 'rep', split_axis=2, concat_axis=0, tiled=True)]
    dynamic_slice x41 -> x0, local copies, waits for them, and re-layouts: 22.1 us -> none  [the longest x40 22.1 us: trimmed_mean(): result = lax.map(lambda item: trimmed_block(item, trim_count), blocks)]
    reduce_sum x41 -> x0, other arithmetic: 15.5 us -> none  [the longest x20 14.3 us: trimmed_block(): rank = jnp.sum((lower | equal).astype(jnp.int32), axis=1)]
    all_to_all x1 -> x0, starting transfers between devices: 13.4 us -> none  [on_device(): lax.all_to_all(grads, 'rep', split_axis=2, concat_axis=0, tiled=True)]
    unnamed x10 -> x7, local copies, waits for them, and re-layouts: 7.62 us -> 3.73 us
  transfers between devices with their start and end apart: 2 -> 0, of which waited for: 2 -> 0; matrix products, arithmetic and copies ran while one was open for 0% -> 0% of each run, Pallas kernels for 0% -> 0%
where the time goes in v1:
time: 85.7 us; the launch traced here: 85.4 us
  Pallas kernels  81 us (95%)
  local copies, waits for them, and re-layouts  3.73 us (4%)
    pallas_call x1, Pallas kernels, on_device(): pl.pallas_call(lambda *refs: kernel(params, *refs), name='robust_step', o...  81 us
    unnamed x7, local copies, waits for them, and re-layouts  3.73 us

profile of v1, /device:TPU:6, one launch (start us, length us, event | category | flops | bytes accessed | tf_op | source)
XLA Modules:
  0.0 85.4 jit_solution(11791352877536616886)
XLA Ops:
  0.6 81.0 %robust_step.1 = (f32[2,4,40,8,128]{4,3,2,1,0:T(8,128)}, f32[2,40,128]{2,1,0:T(8,128)}, f32[2,40,128]{2,1,0:T(8,128)}) custom-call(f32[2,4,40,8,128]{4,3,2,1,0:T(8,128)} %bitcast.13, f32[2,4,40,8,128]{4,3,2,1,0:T(8,128)} %bitcast.14, f32[2,40,128]{2,1,0:T(8,128)} %bitcast.18, f32[2,40,128]{2,1,0:T(8,128)} %bitcast.19), custom_call_target="tpu_custom_call" | custom-call | tf_op jit(solution)/shard_map/robust_step/pallas_call | solution.py:251
  81.7 0.0 copy-start.1
  81.7 0.0 copy-start
  81.7 2.5 %copy.12 = f32[2,32,5120]{2,1,0:T(8,128)} copy(f32[2,32,5120]{2,1,0:T(8,128)} %bitcast.15) | data formatting | bytes 2621440
  84.2 0.0 copy-done.1
  84.2 0.6 copy.13
  84.8 0.0 copy-done
  84.8 0.6 copy.14
Async XLA Ops:
  81.7 2.5 %copy-start.1 = (f32[2,40,128]{2,1,0:T(8,128)S(1)}, f32[2,40,128]{2,1,0:T(8,128)}, u32[]{:S(2)}) copy-start(f32[2,40,128]{2,1,0:T(8,128)} %get-tuple-element.7) | copy-start | bytes 122884
  81.7 3.1 %copy-start = (f32[2,40,128]{2,1,0:T(8,128)S(1)}, f32[2,40,128]{2,1,0:T(8,128)}, u32[]{:S(2)}) copy-start(f32[2,40,128]{2,1,0:T(8,128)} %get-tuple-element.8) | copy-start | bytes 122884

commit v2 on v1

--- a/solution.py
+++ b/solution.py
@@ -7,9 +7,10 @@
 
 STEP = 100
 MESH = pl.DeviceIdType.MESH
-NZ, NX = 8, 4
+NZ, NX, NY = 8, 4, 8
 REPS, SHARDS = 32, 16
 TRIM = 4
+SPLIT = 24
 F32 = jnp.float32
 
 SORT8 = (
@@ -80,13 +81,15 @@
     params,
     grads,
     weight,
-    one_ref,
-    two_ref,
+    moment_one,
+    moment_two,
     new_weight,
     new_one_ref,
     new_two_ref,
     received,
     row,
+    one_ref,
+    two_ref,
     outgoing,
     trimmed,
     partial,
@@ -100,7 +103,12 @@
     z_recv,
     x_recv,
     half_recv,
+    last_recv,
+    four_recv,
     out_sem,
+    above_sem,
+    ring_sem,
+    core_sem,
 ):
     me = lax.axis_index("rep")
     shard = lax.axis_index("shard")
@@ -109,38 +117,92 @@
     def at(dz, dx):
         return lax.rem(z + dz, NZ) * NX + lax.rem(x + dx, NX)
 
-    own_row = pltpu.make_async_copy(row_of(weight, me), row, local_sem.at[0])
-    own_row.start()
-    own_grads = pltpu.make_async_copy(
-        row_of(grads, me), received.at[me], local_sem.at[1]
-    )
-    own_grads.start()
+    y, core = shard // 2, lax.rem(shard, 2)
+
+    def in_y(dy):
+        return lax.rem(y + dy, NY) * 2 + core
+
+    local = [
+        pltpu.make_async_copy(src, dst, local_sem.at[i])
+        for i, (src, dst) in enumerate(
+            (
+                (row_of(grads, me), received.at[me]),
+                (row_of(weight, me), row),
+                (moment_one, one_ref),
+                (moment_two, two_ref),
+            )
+        )
+    ]
+    for copy in local:
+        copy.start()
 
     barrier = pltpu.get_barrier_semaphore()
-    for i in range(1, REPS):
-        pl.semaphore_signal(
-            barrier, inc=1, device_id=(lax.rem(me + i, REPS), shard), device_id_type=MESH
-        )
-    for i in range(1, SHARDS):
-        pl.semaphore_signal(
-            barrier, inc=1, device_id=(me, lax.rem(shard + i, SHARDS)), device_id_type=MESH
-        )
-    pl.semaphore_wait(barrier, REPS + SHARDS - 2)
-
-    for dz in (4, 3, 5, 2, 6, 1, 7, 0):
+
+    def signal(sem, rep, sh):
+        pl.semaphore_signal(sem, inc=1, device_id=(rep, sh), device_id_type=MESH)
+
+    for dx in (2, 1, 3):
+        signal(barrier, at(0, dx), shard)
+    for dy in (1, NY - 1):
+        signal(barrier, me, in_y(dy))
+
+    @pl.when(core == 0)
+    def _():
+        signal(barrier, me, shard + 1)
+
+    pl.semaphore_wait(barrier, 5 + (z > 0).astype(jnp.int32) + core)
+
+    @pl.when(z < NZ - 1)
+    def _():
+        signal(barrier, me + NX, shard)
+
+    @pl.loop(0, z)
+    def _(zz):
+        signal(above_sem.at[z], zz * NX + x, shard)
+
+    def send_grads(zz, dx):
+        peer = zz * NX + lax.rem(x + dx, NX)
+        pltpu.make_async_remote_copy(
+            src_ref=row_of(grads, peer),
+            dst_ref=received.at[me],
+            send_sem=send_sem,
+            recv_sem=recv_sem,
+            device_id=(peer, shard),
+            device_id_type=MESH,
+        ).start()
+
+    @pl.loop(0, z)
+    def _(zz):
         for dx in (2, 1, 3, 0):
-            if dz or dx:
-                peer = at(dz, dx)
-                pltpu.make_async_remote_copy(
-                    src_ref=row_of(grads, peer),
-                    dst_ref=received.at[me],
-                    send_sem=send_sem,
-                    recv_sem=recv_sem,
-                    device_id=(peer, shard),
-                    device_id_type=MESH,
-                ).start()
-    own_row.wait()
-    own_grads.wait()
+            send_grads(zz, dx)
+
+    for dx in (2, 1, 3):
+        send_grads(z, dx)
+
+    @pl.loop(z + 1, NZ)
+    def _(zz):
+        pl.semaphore_wait(above_sem.at[zz], 1)
+        for dx in (2, 1, 3, 0):
+            send_grads(zz, dx)
+
+    @pl.when(core == 0)
+    def _():
+        pl.semaphore_wait(core_sem, 1)
+
+    signal(core_sem, me, shard + 1 - 2 * core)
+
+    @pl.when(core == 1)
+    def _():
+        pl.semaphore_wait(core_sem, 1)
+
+    for r in range(NY // 2 - 1):
+        for side, dy in enumerate((1, NY - 1)):
+            signal(ring_sem.at[r, side], me, in_y(dy))
+        for side in range(2):
+            pl.semaphore_wait(ring_sem.at[r, side], 1)
+
+    for copy in local:
+        copy.wait()
     others = received.at[pl.ds(0, REPS - 1)]
     pltpu.make_async_copy(others, others, recv_sem).wait()
 
@@ -153,12 +215,11 @@
     squares = lax.fori_loop(0, 10, block, jnp.zeros((8, 128), F32))
     total = jnp.sum(squares, axis=0, keepdims=True)
 
-    for stage, (count, mine, device) in enumerate(
-        (
-            (REPS, me, lambda p: (p, shard)),
-            (SHARDS, shard, lambda p: (me, p)),
-        )
-    ):
+    stages = (
+        (2 * REPS, me * 2 + core, lambda p: (p // 2, y * 2 + lax.rem(p, 2))),
+        (NY, y, lambda p: (me, p * 2 + core)),
+    )
+    for stage, (count, mine, device) in enumerate(stages):
         partial[stage] = total
         sums[stage, pl.ds(mine, 1), :] = total
         for i in range(1, count):
@@ -185,61 +246,109 @@
     new_one_ref[...] = new_one
     new_two_ref[...] = new_two
 
-    def at_row(r):
-        return row_of(new_weight, r)
-
-    def push(src, r, peer, sem):
+    first, last = pl.ds(0, SPLIT), pl.ds(SPLIT, 40 - SPLIT)
+    right_left = (1, NX - 1)
+
+    def part(r, tiles):
+        return new_weight.at[:, r // 8, tiles, lax.rem(r, 8), :]
+
+    def half(r, h):
+        return new_weight.at[h, r // 8, first, lax.rem(r, 8), :]
+
+    def four(zz):
+        return new_weight.at[:, zz // 2, last, pl.ds(lax.rem(zz, 2) * 4, 4), :]
+
+    def half_four(zz, h):
+        return new_weight.at[h, zz // 2, last, pl.ds(lax.rem(zz, 2) * 4, 4), :]
+
+    def push(src, dst, peer, sem):
         pltpu.make_async_remote_copy(
             src_ref=src,
-            dst_ref=at_row(r),
+            dst_ref=dst,
             send_sem=gather_send,
             recv_sem=sem,
             device_id=(peer, shard),
             device_id_type=MESH,
         ).start()
 
-    for dz in (1, 7, 2, 6, 3, 5, 4):
-        push(outgoing, me, at(dz, 0), z_recv.at[z])
-    for side, dx in enumerate((1, 3)):
-        push(outgoing, me, at(0, dx), x_recv.at[side, z])
-    keep = pltpu.make_async_copy(outgoing, at_row(me), out_sem)
+    def came(view, sem):
+        pltpu.make_async_copy(view, view, sem).wait()
+
+    def zs(dz):
+        return lax.rem(z + dz, NZ)
+
+    def along_x(dz, src=None):
+        view = part(at(dz, 0), first)
+        for side, dx in enumerate(right_left):
+            push(view if src is None else src, view, at(0, dx), x_recv.at[side, zs(dz)])
+
+    def relay_x(dz):
+        for side, dx in enumerate(right_left):
+            r = at(dz, NX - dx)
+            came(part(r, first), x_recv.at[side, zs(dz)])
+            push(half(r, side), half(r, side), at(0, dx), half_recv)
+
+    def from_z(dz):
+        came(part(at(dz, 0), first), z_recv.at[zs(dz)])
+
+    own_first, own_last = outgoing.at[:, first, :], outgoing.at[:, last, :]
+    for dz in (2, 6, 1, 7):
+        push(own_first, part(me, first), at(dz, 0), z_recv.at[z])
+    along_x(0, own_first)
+    for dx in (2, 1, 3):
+        push(own_last, part(me, last), at(0, dx), last_recv)
+    keep = pltpu.make_async_copy(outgoing, row_of(new_weight, me), out_sem)
     keep.start()
 
-    def from_x(dz):
-        zz = lax.rem(z + dz, NZ)
-        for side, dx in enumerate((1, 3)):
-            r = at(dz, NX - dx)
-            view = at_row(r)
-            pltpu.make_async_copy(view, view, x_recv.at[side, zz]).wait()
-            half = new_weight.at[side, r // 8, :, lax.rem(r, 8), :]
-            pltpu.make_async_remote_copy(
-                src_ref=half,
-                dst_ref=half,
-                send_sem=gather_send,
-                recv_sem=half_recv,
-                device_id=(at(0, dx), shard),
-                device_id_type=MESH,
-            ).start()
-
-    order = (0, 1, 7, 2, 6, 3, 5, 4)
-    for k, dz in enumerate(order[1:]):
-        zz = lax.rem(z + dz, NZ)
-        r = at(dz, 0)
-        view = at_row(r)
-        pltpu.make_async_copy(view, view, z_recv.at[zz]).wait()
-        for side, dx in enumerate((1, 3)):
-            push(view, r, at(0, dx), x_recv.at[side, zz])
-        from_x(order[k])
-    from_x(order[-1])
-    eight = received.at[pl.ds(0, 8)]
-    pltpu.make_async_copy(eight, eight, half_recv).wait()
+    for dz in (1, 7):
+        from_z(dz)
+        along_x(dz)
+    for dz, on in ((6, 1), (2, 7)):
+        from_z(dz)
+        r, h = at(dz, 0), (0 if on == 1 else 1)
+        push(part(r, first), part(r, first), at(on, 0), z_recv.at[zs(dz)])
+        push(half(r, h), half(r, h), at(2 * on % NZ, 0), z_recv.at[zs(dz)])
+        along_x(dz)
+    relay_x(0)
+    three = received.at[pl.ds(0, 3), :, last, :]
+    came(three, last_recv)
     keep.wait()
+    for dz in (2, 6, 1, 7):
+        push(four(z), four(z), at(dz, 0), four_recv.at[z])
+    for dz in (1, 7, 2, 6):
+        relay_x(dz)
+    for dz in (3, 5, 4):
+        from_z(dz)
+        along_x(dz)
+    for dz, on in ((6, 1), (2, 7)):
+        zz, h = zs(dz), (0 if on == 1 else 1)
+        came(four(zz), four_recv.at[zz])
+        push(four(zz), four(zz), at(on, 0), four_recv.at[zz])
+        push(half_four(zz, h), half_four(zz, h), at(2 * on % NZ, 0), four_recv.at[zz])
+    for dz in (3, 5, 4):
+        relay_x(dz)
+    for dz in (1, 7, 3, 5, 4):
+        came(four(zs(dz)), four_recv.at[zs(dz)])
+    came(received.at[pl.ds(0, 8), :, first, :], half_recv)
 
     pltpu.make_async_copy(others, others, send_sem).wait()
     pltpu.make_async_copy(others, others, gather_send).wait()
-    for stage, count in enumerate((REPS, SHARDS)):
+    for stage, (count, _, _) in enumerate(stages):
         got = sums.at[stage, pl.ds(0, count - 1), :]
         pltpu.make_async_copy(got, got, sum_send.at[stage]).wait()
+
+
+def store(*refs):
+    *pairs, sems = refs
+    copies = [pltpu.make_async_copy(pairs[i], pairs[i + 3], sems.at[i]) for i in range(3)]
+    for copy in copies:
+        copy.start()
+    for copy in copies:
+        copy.wait()
+
+
+def pinned(array):
+    return pltpu.with_memory_space_constraint(array, pltpu.HBM)
 
 
 def on_device(grads, weight, moment_one, moment_two):
@@ -247,25 +356,27 @@
     vmem = pl.BlockSpec(memory_space=pltpu.VMEM)
     hbm = pl.BlockSpec(memory_space=pltpu.HBM)
     unit = (2, 40, 128)
-    dma = pltpu.SemaphoreType.DMA
-    new_weight, new_one, new_two = pl.pallas_call(
+    dma, regular = pltpu.SemaphoreType.DMA, pltpu.SemaphoreType.REGULAR
+    results = pl.pallas_call(
         lambda *refs: kernel(params, *refs),
         name="robust_step",
         out_shape=(
-            jax.ShapeDtypeStruct((2, 4, 40, 8, 128), F32),
-            jax.ShapeDtypeStruct(unit, F32),
-            jax.ShapeDtypeStruct(unit, F32),
+            pltpu.VMEM((2, 4, 40, 8, 128), F32),
+            pltpu.VMEM(unit, F32),
+            pltpu.VMEM(unit, F32),
         ),
-        in_specs=[hbm, hbm, vmem, vmem],
+        in_specs=[hbm] * 4,
         out_specs=(vmem, vmem, vmem),
         scratch_shapes=[
             pltpu.VMEM((REPS,) + unit, F32),
             pltpu.VMEM(unit, F32),
             pltpu.VMEM(unit, F32),
             pltpu.VMEM(unit, F32),
+            pltpu.VMEM(unit, F32),
+            pltpu.VMEM(unit, F32),
             pltpu.VMEM((2, 1, 128), F32),
-            pltpu.VMEM((2, REPS, 128), F32),
-            dma((2,)),
+            pltpu.VMEM((2, 2 * REPS, 128), F32),
+            dma((4,)),
             dma,
             dma,
             dma((2,)),
@@ -275,11 +386,25 @@
             dma((2, NZ)),
             dma,
             dma,
+            dma((NZ,)),
+            dma,
+            regular((NZ,)),
+            regular((NY // 2 - 1, 2)),
+            regular,
         ],
         compiler_params=pltpu.CompilerParams(
-            collective_id=0, has_side_effects=True
+            collective_id=0, has_side_effects=True, vmem_limit_bytes=32 << 20
         ),
-    )(tiles(grads[0]), tiles(weight), moment_one.reshape(unit), moment_two.reshape(unit))
+    )(pinned(tiles(grads[0])), pinned(tiles(weight)), pinned(moment_one.reshape(unit)), pinned(moment_two.reshape(unit)))
+    new_weight, new_one, new_two = pl.pallas_call(
+        store,
+        name="store",
+        out_shape=tuple(jax.ShapeDtypeStruct(r.shape, F32) for r in results),
+        in_specs=[vmem] * 3,
+        out_specs=(hbm,) * 3,
+        scratch_shapes=[dma((3,))],
+        compiler_params=pltpu.CompilerParams(vmem_limit_bytes=16 << 20),
+    )(*results)
     return (
         new_weight.transpose(0, 1, 3, 2, 4).reshape(weight.shape),
         new_one.reshape(moment_one.shape),

time: 85.7 us -> 74.3 us (0.87)
  Pallas kernels: 81 us -> 72.7 us
  local copies, waits for them, and re-layouts: 3.73 us -> 0 us
    pallas_call x1, Pallas kernels: 81 us -> 71.6 us  [on_device(): pl.pallas_call(lambda *refs: kernel(params, *refs), name='robust_step', o...]
    unnamed x7 -> x0, local copies, waits for them, and re-layouts: 3.73 us -> none
    pallas_call x0 -> x1, Pallas kernels: none -> 1.09 us  [on_device(): pl.pallas_call(store, name='store', out_shape=tuple((jax.ShapeDtypeStruct...]
where the time goes in v2:
time: 74.3 us; the launch traced here: 73.4 us
  Pallas kernels  72.7 us (98%)
    pallas_call x1, Pallas kernels, on_device(): pl.pallas_call(lambda *refs: kernel(params, *refs), name='robust_step', o...  71.6 us

profile of v2, /device:TPU:6, one launch (start us, length us, event | category | flops | bytes accessed | tf_op | source)
XLA Modules:
  0.0 73.4 jit_solution(1417301219736306655)
XLA Ops:
  0.6 71.6 %robust_step.1 = (f32[2,4,40,8,128]{4,3,2,1,0:T(8,128)S(1)}, f32[2,40,128]{2,1,0:T(8,128)S(1)}, f32[2,40,128]{2,1,0:T(8,128)S(1)}) custom-call(f32[2,4,40,8,128]{4,3,2,1,0:T(8,128)} %bitcast.13, f32[2,4,40,8,128]{4,3,2,1,0:T(8,128)} %bitcast.14, f32[2,40,128]{2,1,0:T(8,128)} %bitcast.15, f32[2,40,128]{2,1,0:T(8,128)} %bitcast.16), custom_call_target="tpu_custom_call" | custom-call | tf_op jit(solution)/shard_map/robust_step/pallas_call | solution.py:360
  72.3 1.1 %store.1 = (f32[2,4,40,8,128]{4,3,2,1,0:T(8,128)}, f32[2,40,128]{2,1,0:T(8,128)}, f32[2,40,128]{2,1,0:T(8,128)}) custom-call(f32[2,4,40,8,128]{4,3,2,1,0:T(8,128)S(1)} %get-tuple-element.9.refs_0_, f32[2,40,128]{2,1,0:T(8,128)S(1)} %get-tuple-element.10.refs_1_, f32[2,40,128]{2,1,0:T(8,128)S(1)} %get-tuple-element.11.refs_2_), custom_call_target="tpu_custom_call" | custom-call | tf_op jit(solution)/shard_map/store/pallas_call | solution.py:399

commit v3 on v2

--- a/solution.py
+++ b/solution.py
@@ -62,15 +62,20 @@
     )
 
 
-def kept_sum(values):
-    groups = [sort8(values[8 * g : 8 * g + 8]) for g in range(4)]
-    left, left_sum = merge(groups[0], groups[1])
-    right, right_sum = merge(groups[2], groups[3])
-    return left_sum + right_sum + middle(left, right)
-
-
 def row_of(ref, r):
     return ref.at[:, r // 8, :, lax.rem(r, 8), :]
+
+
+def half_row(ref, r, h):
+    return ref.at[h, r // 8, :, lax.rem(r, 8), :]
+
+
+def bundle(h, slot):
+    return h * 16 + slot
+
+
+def direct(h, slot):
+    return REPS + h * 16 + slot
 
 
 def tiles(block):
@@ -87,6 +92,7 @@
     new_one_ref,
     new_two_ref,
     received,
+    summary,
     row,
     one_ref,
     two_ref,
@@ -96,7 +102,10 @@
     sums,
     local_sem,
     send_sem,
+    bundle_recv,
     recv_sem,
+    summary_send,
+    summary_recv,
     sum_send,
     sum_recv,
     gather_send,
@@ -126,7 +135,10 @@
         pltpu.make_async_copy(src, dst, local_sem.at[i])
         for i, (src, dst) in enumerate(
             (
-                (row_of(grads, me), received.at[me]),
+                (half_row(grads, me, 0), received.at[direct(0, x)]),
+                (half_row(grads, me, 1), received.at[direct(1, x)]),
+                (half_row(grads, at(NZ - 1, 0), 0), received.at[bundle(0, x)]),
+                (half_row(grads, at(1, 0), 1), received.at[bundle(1, x)]),
                 (row_of(weight, me), row),
                 (moment_one, one_ref),
                 (moment_two, two_ref),
@@ -160,30 +172,60 @@
     def _(zz):
         signal(above_sem.at[z], zz * NX + x, shard)
 
-    def send_grads(zz, dx):
-        peer = zz * NX + lax.rem(x + dx, NX)
+    def send_half(row_index, h, slot, peer, sem):
         pltpu.make_async_remote_copy(
-            src_ref=row_of(grads, peer),
-            dst_ref=received.at[me],
+            src_ref=half_row(grads, row_index, h),
+            dst_ref=received.at[slot],
             send_sem=send_sem,
-            recv_sem=recv_sem,
+            recv_sem=sem,
             device_id=(peer, shard),
             device_id_type=MESH,
         ).start()
 
-    @pl.loop(0, z)
-    def _(zz):
-        for dx in (2, 1, 3, 0):
-            send_grads(zz, dx)
+    def towards(zz):
+        d = lax.rem(zz - z + NZ, NZ)
+        down = (d > NZ // 2).astype(jnp.int32)
+        distance = d + down * (NZ - 2 * d)
+        return down, distance, d != NZ // 2
+
+    def send_bundles(zz):
+        down, distance, far = towards(zz)
+        beyond = lax.rem(zz + 1 + down * (NZ - 2), NZ)
+
+        @pl.when(far)
+        def _():
+            for dx in (2, 1, 3, 0):
+                xx = lax.rem(x + dx, NX)
+                slot = bundle(1 - down, distance * NX + x)
+                send_half(beyond * NX + xx, 1 - down, slot, zz * NX + xx, bundle_recv.at[1 - down])
+
+    def send_direct(zz):
+        down, distance, far = towards(zz)
+
+        @pl.when(far)
+        def _():
+            for dx in (2, 1, 3, 0):
+                xx = lax.rem(x + dx, NX)
+                slot = direct(down, distance * NX + x)
+                send_half(zz * NX + xx, down, slot, zz * NX + xx, recv_sem)
+
+    pl.loop(0, z)(send_bundles)
 
     for dx in (2, 1, 3):
-        send_grads(z, dx)
+        send_half(at(NZ - 1, dx), 0, bundle(0, x), at(0, dx), bundle_recv.at[0])
+        send_half(at(1, dx), 1, bundle(1, x), at(0, dx), bundle_recv.at[1])
+
+    pl.loop(0, z)(send_direct)
+
+    for dx in (2, 1, 3):
+        for h in range(2):
+            send_half(at(0, dx), h, direct(h, x), at(0, dx), recv_sem)
 
     @pl.loop(z + 1, NZ)
     def _(zz):
         pl.semaphore_wait(above_sem.at[zz], 1)
-        for dx in (2, 1, 3, 0):
-            send_grads(zz, dx)
+        send_bundles(zz)
+        send_direct(zz)
 
     @pl.when(core == 0)
     def _():
@@ -203,12 +245,44 @@
 
     for copy in local:
         copy.wait()
-    others = received.at[pl.ds(0, REPS - 1)]
-    pltpu.make_async_copy(others, others, recv_sem).wait()
+    def came(view, sem):
+        pltpu.make_async_copy(view, view, sem).wait()
+
+    def halves(n):
+        return received.at[pl.ds(0, n)]
+
+    def condense(first_slot):
+        @pl.loop(0, 5)
+        def _(j):
+            rows = pl.ds(pl.multiple_of(j * 8, 8), 8)
+            values = [received[first_slot + i, rows, :] for i in range(16)]
+            (low, high), rest = merge(sort8(values[:8]), sort8(values[8:]))
+            for i, value in enumerate(low + high + [rest]):
+                received[first_slot + i, rows, :] = value
+
+    for h, dz in enumerate((NZ - 1, 1)):
+        came(halves(15), bundle_recv.at[h])
+        condense(bundle(h, 0))
+        pltpu.make_async_remote_copy(
+            src_ref=received.at[pl.ds(bundle(h, 0), 9)],
+            dst_ref=summary.at[h],
+            send_sem=summary_send,
+            recv_sem=summary_recv.at[h],
+            device_id=(at(dz, 0), shard),
+            device_id_type=MESH,
+        ).start()
+    came(halves(30), recv_sem)
+    for h in range(2):
+        condense(direct(h, 0))
+    for h in range(2):
+        came(halves(9), summary_recv.at[h])
 
     def block(j, squares):
         h, rows = j // 5, pl.ds(pl.multiple_of(lax.rem(j, 5) * 8, 8), 8)
-        mean = kept_sum([received[i, h, rows, :] for i in range(REPS)]) / (REPS - 2 * TRIM)
+        near = [received[direct(h, i), rows, :] for i in range(9)]
+        far = [summary[h, i, rows, :] for i in range(9)]
+        rest = middle((near[:4], near[4:8]), (far[:4], far[4:8]))
+        mean = (near[8] + far[8] + rest) / (REPS - 2 * TRIM)
         trimmed[h, rows, :] = mean
         return squares + mean * mean
 
@@ -271,9 +345,6 @@
             device_id_type=MESH,
         ).start()
 
-    def came(view, sem):
-        pltpu.make_async_copy(view, view, sem).wait()
-
     def zs(dz):
         return lax.rem(z + dz, NZ)
 
@@ -310,7 +381,7 @@
         push(half(r, h), half(r, h), at(2 * on % NZ, 0), z_recv.at[zs(dz)])
         along_x(dz)
     relay_x(0)
-    three = received.at[pl.ds(0, 3), :, last, :]
+    three = received.at[pl.ds(0, 6), last, :]
     came(three, last_recv)
     keep.wait()
     for dz in (2, 6, 1, 7):
@@ -329,10 +400,11 @@
         relay_x(dz)
     for dz in (1, 7, 3, 5, 4):
         came(four(zs(dz)), four_recv.at[zs(dz)])
-    came(received.at[pl.ds(0, 8), :, first, :], half_recv)
-
-    pltpu.make_async_copy(others, others, send_sem).wait()
-    pltpu.make_async_copy(others, others, gather_send).wait()
+    came(received.at[pl.ds(0, 16), first, :], half_recv)
+
+    came(halves(60), send_sem)
+    came(halves(18), summary_send)
+    came(halves(62), gather_send)
     for stage, (count, _, _) in enumerate(stages):
         got = sums.at[stage, pl.ds(0, count - 1), :]
         pltpu.make_async_copy(got, got, sum_send.at[stage]).wait()
@@ -368,7 +440,8 @@
         in_specs=[hbm] * 4,
         out_specs=(vmem, vmem, vmem),
         scratch_shapes=[
-            pltpu.VMEM((REPS,) + unit, F32),
+            pltpu.VMEM((2 * REPS, 40, 128), F32),
+            pltpu.VMEM((2, 9, 40, 128), F32),
             pltpu.VMEM(unit, F32),
             pltpu.VMEM(unit, F32),
             pltpu.VMEM(unit, F32),
@@ -376,9 +449,12 @@
             pltpu.VMEM(unit, F32),
             pltpu.VMEM((2, 1, 128), F32),
             pltpu.VMEM((2, 2 * REPS, 128), F32),
-            dma((4,)),
-            dma,
-            dma,
+            dma((7,)),
+            dma,
+            dma((2,)),
+            dma,
+            dma,
+            dma((2,)),
             dma((2,)),
             dma((2,)),
             dma,

time: 74.3 us -> 71.8 us (0.966)
  Pallas kernels: 72.7 us -> 71 us
    pallas_call x1, Pallas kernels: 71.6 us -> 69.9 us  [on_device(): pl.pallas_call(lambda *refs: kernel(params, *refs), name='robust_step', o...]
where the time goes in v3:
time: 71.8 us; the launch traced here: 71.6 us
  Pallas kernels  71 us (99%)
    pallas_call x1, Pallas kernels, on_device(): pl.pallas_call(lambda *refs: kernel(params, *refs), name='robust_step', o...  69.9 us

profile of v3, /device:TPU:6, one launch (start us, length us, event | category | flops | bytes accessed | tf_op | source)
XLA Modules:
  0.0 71.6 jit_solution(13594897939042370666)
XLA Ops:
  0.6 69.9 %robust_step.1 = (f32[2,4,40,8,128]{4,3,2,1,0:T(8,128)S(1)}, f32[2,40,128]{2,1,0:T(8,128)S(1)}, f32[2,40,128]{2,1,0:T(8,128)S(1)}) custom-call(f32[2,4,40,8,128]{4,3,2,1,0:T(8,128)} %bitcast.13, f32[2,4,40,8,128]{4,3,2,1,0:T(8,128)} %bitcast.14, f32[2,40,128]{2,1,0:T(8,128)} %bitcast.15, f32[2,40,128]{2,1,0:T(8,128)} %bitcast.16), custom_call_target="tpu_custom_call" | custom-call | tf_op jit(solution)/shard_map/robust_step/pallas_call | solution.py:432
  70.5 1.1 %store.1 = (f32[2,4,40,8,128]{4,3,2,1,0:T(8,128)}, f32[2,40,128]{2,1,0:T(8,128)}, f32[2,40,128]{2,1,0:T(8,128)}) custom-call(f32[2,4,40,8,128]{4,3,2,1,0:T(8,128)S(1)} %get-tuple-element.9.refs_0_, f32[2,40,128]{2,1,0:T(8,128)S(1)} %get-tuple-element.10.refs_1_, f32[2,40,128]{2,1,0:T(8,128)S(1)} %get-tuple-element.11.refs_2_), custom_call_target="tpu_custom_call" | custom-call | tf_op jit(solution)/shard_map/store/pallas_call | solution.py:475

commit v4 on v3

--- a/solution.py
+++ b/solution.py
@@ -145,8 +145,6 @@
             )
         )
     ]
-    for copy in local:
-        copy.start()
 
     barrier = pltpu.get_barrier_semaphore()
 
@@ -162,11 +160,12 @@
     def _():
         signal(barrier, me, shard + 1)
 
-    pl.semaphore_wait(barrier, 5 + (z > 0).astype(jnp.int32) + core)
-
-    @pl.when(z < NZ - 1)
-    def _():
-        signal(barrier, me + NX, shard)
+    @pl.loop(z + 1, NZ)
+    def _(zz):
+        for xx in range(NX):
+            signal(barrier, zz * NX + xx, shard)
+
+    pl.semaphore_wait(barrier, 5 + NX * z + core)
 
     @pl.loop(0, z)
     def _(zz):
@@ -225,7 +224,11 @@
     def _(zz):
         pl.semaphore_wait(above_sem.at[zz], 1)
         send_bundles(zz)
-        send_direct(zz)
+
+    pl.loop(z + 1, NZ)(send_direct)
+
+    for copy in local:
+        copy.start()
 
     @pl.when(core == 0)
     def _():

time: 71.8 us -> 69.6 us (0.969)
  Pallas kernels: 71 us -> 68.7 us
    pallas_call x1, Pallas kernels: 69.9 us -> 67.6 us  [on_device(): pl.pallas_call(lambda *refs: kernel(params, *refs), name='robust_step', o...]
where the time goes in v4:
time: 69.6 us; the launch traced here: 69.3 us
  Pallas kernels  68.7 us (99%)
    pallas_call x1, Pallas kernels, on_device(): pl.pallas_call(lambda *refs: kernel(params, *refs), name='robust_step', o...  67.6 us

profile of v4, /device:TPU:6, one launch (start us, length us, event | category | flops | bytes accessed | tf_op | source)
XLA Modules:
  0.0 69.3 jit_solution(15854171047327511654)
XLA Ops:
  0.6 67.6 %robust_step.1 = (f32[2,4,40,8,128]{4,3,2,1,0:T(8,128)S(1)}, f32[2,40,128]{2,1,0:T(8,128)S(1)}, f32[2,40,128]{2,1,0:T(8,128)S(1)}) custom-call(f32[2,4,40,8,128]{4,3,2,1,0:T(8,128)} %bitcast.13, f32[2,4,40,8,128]{4,3,2,1,0:T(8,128)} %bitcast.14, f32[2,40,128]{2,1,0:T(8,128)} %bitcast.15, f32[2,40,128]{2,1,0:T(8,128)} %bitcast.16), custom_call_target="tpu_custom_call" | custom-call | tf_op jit(solution)/shard_map/robust_step/pallas_call | solution.py:435
  68.3 1.1 %store.1 = (f32[2,4,40,8,128]{4,3,2,1,0:T(8,128)}, f32[2,40,128]{2,1,0:T(8,128)}, f32[2,40,128]{2,1,0:T(8,128)}) custom-call(f32[2,4,40,8,128]{4,3,2,1,0:T(8,128)S(1)} %get-tuple-element.9.refs_0_, f32[2,40,128]{2,1,0:T(8,128)S(1)} %get-tuple-element.10.refs_1_, f32[2,40,128]{2,1,0:T(8,128)S(1)} %get-tuple-element.11.refs_2_), custom_call_target="tpu_custom_call" | custom-call | tf_op jit(solution)/shard_map/store/pallas_call | solution.py:478

commit v5 on v4

--- a/solution.py
+++ b/solution.py
@@ -225,7 +225,11 @@
         pl.semaphore_wait(above_sem.at[zz], 1)
         send_bundles(zz)
 
-    pl.loop(z + 1, NZ)(send_direct)
+        @pl.when(zz - 1 > z)
+        def _():
+            send_direct(zz - 1)
+
+    pl.loop(jnp.maximum(z + 1, NZ - 1), NZ)(send_direct)
 
     for copy in local:
         copy.start()
@@ -389,11 +393,11 @@
     keep.wait()
     for dz in (2, 6, 1, 7):
         push(four(z), four(z), at(dz, 0), four_recv.at[z])
-    for dz in (1, 7, 2, 6):
-        relay_x(dz)
     for dz in (3, 5, 4):
         from_z(dz)
         along_x(dz)
+    for dz in (1, 7, 2, 6):
+        relay_x(dz)
     for dz, on in ((6, 1), (2, 7)):
         zz, h = zs(dz), (0 if on == 1 else 1)
         came(four(zz), four_recv.at[zz])

time: 69.6 us -> 69.5 us (level)
  no operation moved by 1% of the time
where the time goes in v5:
time: 69.5 us; the launch traced here: 69.4 us
  Pallas kernels  68.8 us (99%)
    pallas_call x1, Pallas kernels, on_device(): pl.pallas_call(lambda *refs: kernel(params, *refs), name='robust_step', o...  67.7 us

profile of v5, /device:TPU:6, one launch (start us, length us, event | category | flops | bytes accessed | tf_op | source)
XLA Modules:
  0.0 69.4 jit_solution(10930017425154984004)
XLA Ops:
  0.6 67.7 %robust_step.1 = (f32[2,4,40,8,128]{4,3,2,1,0:T(8,128)S(1)}, f32[2,40,128]{2,1,0:T(8,128)S(1)}, f32[2,40,128]{2,1,0:T(8,128)S(1)}) custom-call(f32[2,4,40,8,128]{4,3,2,1,0:T(8,128)} %bitcast.13, f32[2,4,40,8,128]{4,3,2,1,0:T(8,128)} %bitcast.14, f32[2,40,128]{2,1,0:T(8,128)} %bitcast.15, f32[2,40,128]{2,1,0:T(8,128)} %bitcast.16), custom_call_target="tpu_custom_call" | custom-call | tf_op jit(solution)/shard_map/robust_step/pallas_call | solution.py:439
  68.3 1.1 %store.1 = (f32[2,4,40,8,128]{4,3,2,1,0:T(8,128)}, f32[2,40,128]{2,1,0:T(8,128)}, f32[2,40,128]{2,1,0:T(8,128)}) custom-call(f32[2,4,40,8,128]{4,3,2,1,0:T(8,128)S(1)} %get-tuple-element.9.refs_0_, f32[2,40,128]{2,1,0:T(8,128)S(1)} %get-tuple-element.10.refs_1_, f32[2,40,128]{2,1,0:T(8,128)S(1)} %get-tuple-element.11.refs_2_), custom_call_target="tpu_custom_call" | custom-call | tf_op jit(solution)/shard_map/store/pallas_call | solution.py:482

commit v6 on v5

--- a/solution.py
+++ b/solution.py
@@ -366,6 +366,14 @@
             came(part(r, first), x_recv.at[side, zs(dz)])
             push(half(r, side), half(r, side), at(0, dx), half_recv)
 
+    def across_x(dz):
+        view = part(at(dz, 0), first)
+        push(view, view, at(0, 2), half_recv)
+
+    def arrive_x(dz):
+        for side, dx in enumerate(right_left):
+            came(part(at(dz, NX - dx), first), x_recv.at[side, zs(dz)])
+
     def from_z(dz):
         came(part(at(dz, 0), first), z_recv.at[zs(dz)])
 
@@ -395,6 +403,8 @@
         push(four(z), four(z), at(dz, 0), four_recv.at[z])
     for dz in (3, 5, 4):
         from_z(dz)
+        if dz == 4:
+            across_x(dz)
         along_x(dz)
     for dz in (1, 7, 2, 6):
         relay_x(dz)
@@ -403,8 +413,9 @@
         came(four(zz), four_recv.at[zz])
         push(four(zz), four(zz), at(on, 0), four_recv.at[zz])
         push(half_four(zz, h), half_four(zz, h), at(2 * on % NZ, 0), four_recv.at[zz])
-    for dz in (3, 5, 4):
+    for dz in (3, 5):
         relay_x(dz)
+    arrive_x(4)
     for dz in (1, 7, 3, 5, 4):
         came(four(zs(dz)), four_recv.at[zs(dz)])
     came(received.at[pl.ds(0, 16), first, :], half_recv)

time: 69.5 us -> 69.5 us (level)
  no operation moved by 1% of the time
where the time goes in v6:
time: 69.5 us; the launch traced here: 69.4 us
  Pallas kernels  68.8 us (99%)
    pallas_call x1, Pallas kernels, on_device(): pl.pallas_call(lambda *refs: kernel(params, *refs), name='robust_step', o...  67.7 us

profile of v6, /device:TPU:6, one launch (start us, length us, event | category | flops | bytes accessed | tf_op | source)
XLA Modules:
  0.0 69.4 jit_solution(1853981852081850972)
XLA Ops:
  0.6 67.7 %robust_step.1 = (f32[2,4,40,8,128]{4,3,2,1,0:T(8,128)S(1)}, f32[2,40,128]{2,1,0:T(8,128)S(1)}, f32[2,40,128]{2,1,0:T(8,128)S(1)}) custom-call(f32[2,4,40,8,128]{4,3,2,1,0:T(8,128)} %bitcast.13, f32[2,4,40,8,128]{4,3,2,1,0:T(8,128)} %bitcast.14, f32[2,40,128]{2,1,0:T(8,128)} %bitcast.15, f32[2,40,128]{2,1,0:T(8,128)} %bitcast.16), custom_call_target="tpu_custom_call" | custom-call | tf_op jit(solution)/shard_map/robust_step/pallas_call | solution.py:450
  68.3 1.1 %store.1 = (f32[2,4,40,8,128]{4,3,2,1,0:T(8,128)}, f32[2,40,128]{2,1,0:T(8,128)}, f32[2,40,128]{2,1,0:T(8,128)}) custom-call(f32[2,4,40,8,128]{4,3,2,1,0:T(8,128)S(1)} %get-tuple-element.9.refs_0_, f32[2,40,128]{2,1,0:T(8,128)S(1)} %get-tuple-element.10.refs_1_, f32[2,40,128]{2,1,0:T(8,128)S(1)} %get-tuple-element.11.refs_2_), custom_call_target="tpu_custom_call" | custom-call | tf_op jit(solution)/shard_map/store/pallas_call | solution.py:493
